TPU v7x, 256 devices: a whole 4x4x8 slice. The times are simulated.
256 devices in a mesh: section: 4 (over z_lo), rep: 8 (over y, core), tp: 8 (over z_hi, x).
Axes of the slice: x: 4, y: 4, z: 8 (z_hi: 2, z_lo: 4; z = z_hi * 4 + z_lo), core: 2. Of those that a mesh axis runs over, the one named last changes fastest.
Arguments:
- acts: bfloat16 [8, 256, 896], P('rep', None, 'tp'), may hold values from -6 to 6
- cotangent: bfloat16 [8, 256, 896], P('rep', None, 'tp'), may hold values from -8.5 to 8.5
- w_gate: bfloat16 [4, 8, 896, 4864], P('section', 'rep', None, 'tp'), may hold values from -3 to 3
- w_up: bfloat16 [4, 8, 896, 4864], P('section', 'rep', None, 'tp'), may hold values from -3 to 3
- w_down: bfloat16 [4, 8, 4864, 896], P('section', 'rep', 'tp'), may hold values from -4.2 to 4.2
- m_gate: bfloat16 [4, 8, 896, 4864], P('section', 'rep', None, 'tp'), may hold values from -0.099609375 to 0.099609375
- m_up: bfloat16 [4, 8, 896, 4864], P('section', 'rep', None, 'tp'), may hold values from -0.099609375 to 0.099609375
- m_down: bfloat16 [4, 8, 4864, 896], P('section', 'rep', 'tp'), may hold values from -0.099609375 to 0.099609375
- v_gate: bfloat16 [4, 8, 896, 4864], P('section', 'rep', None, 'tp'), may hold values from 0.0009994507 to 0.099609375
- v_up: bfloat16 [4, 8, 896, 4864], P('section', 'rep', None, 'tp'), may hold values from 0.0009994507 to 0.099609375
- v_down: bfloat16 [4, 8, 4864, 896], P('section', 'rep', 'tp'), may hold values from 0.0009994507 to 0.099609375
- steps: int32 [4], P('section'), may hold values from 0 to 999
Outputs:
- section_out: bfloat16 [4, 8, 256, 896], P('section', 'rep', None, 'tp')
- section_in_grad: bfloat16 [4, 8, 256, 896], P('section', 'rep', None, 'tp')
- new_gate: bfloat16 [4, 8, 896, 4864], P('section', 'rep', None, 'tp')
- new_up: bfloat16 [4, 8, 896, 4864], P('section', 'rep', None, 'tp')
- new_down: bfloat16 [4, 8, 4864, 896], P('section', 'rep', 'tp')
All inputs are finite; a program needn't handle non-finite values.
Results may differ from a plain program's by a relative error of at most 0.023.
Values may be sent and summed in bfloat16 or wider, within the bound.
A program may use at most 128 MiB of HBM per device.

v0:
```python
import functools
import math

import jax
import jax.numpy as jnp
from jax import lax
from jax.sharding import PartitionSpec as P

D = 896
FF = 4864
TOK = 128
MB = 2


NORM_EPS = 1e-06
ADAM_EPS = 1e-08
LEARN = 0.3
BETA_ONE = 0.9
BETA_TWO = 0.95


def as_sent(array):
    return jax.tree.map(lambda a: a.astype(jnp.bfloat16) if a.dtype == jnp.float32 else a, array)


def from_behind(array, axis, by):
    peers = lax.axis_size(axis)
    return lax.ppermute(array, axis, [(i, (i + by) % peers) for i in range(peers)])


def passed_along(value, axis, steps):
    count = lax.axis_size(axis)
    first, last = (max(0, -steps), min(count, count - steps))
    return lax.ppermute(value, axis, [(source, source + steps) for source in range(first, last)])


def widen(value):
    return lax.all_gather(value, "tp", axis=1, tiled=True)


def norm_parts(x_full):
    xf = x_full.astype(jnp.float32)
    rms = jnp.sqrt(jnp.mean(xf * xf, axis=1, keepdims=True) + NORM_EPS)
    normed = xf / rms
    normed_b = normed.astype(jnp.bfloat16)
    return (xf, rms, normed, normed_b)


def forward_parts(x_full, wg, wu):
    xf, rms, normed, normed_b = norm_parts(x_full)
    gate = jnp.dot(normed_b, wg, preferred_element_type=jnp.float32) * (1.0 / math.sqrt(D))
    upper = jnp.dot(normed_b, wu, preferred_element_type=jnp.float32) * (1.0 / math.sqrt(D))
    return (xf, rms, normed, normed_b, gate, upper)


def adam_step(weight, first, second, grad):
    m_new = BETA_ONE * first.astype(jnp.float32) + (1.0 - BETA_ONE) * grad
    v_new = BETA_TWO * second.astype(jnp.float32) + (1.0 - BETA_TWO) * grad * grad
    return (weight.astype(jnp.float32) - LEARN * m_new / (jnp.sqrt(v_new) + ADAM_EPS)).astype(
        jnp.bfloat16
    )


def partner_mean(stacked, distance):
    other = jax.tree.map(
        lambda part, own: part.astype(own.dtype),
        from_behind(as_sent(stacked), "rep", distance),
        stacked,
    )
    return ((stacked.astype(jnp.float32) + other.astype(jnp.float32)) * 0.5).astype(jnp.bfloat16)


def contract(left, right, left_dim, right_dim):
    return lax.dot_general(
        left, right, (((left_dim,), (right_dim,)), ((), ())), preferred_element_type=jnp.float32
    )


def on_device(
    acts, cotangent, w_gate, w_up, w_down, m_gate, m_up, m_down, v_gate, v_up, v_down, steps
):
    section = lax.axis_index("section")
    sections = lax.axis_size("section")
    part = lax.axis_index("tp")
    local_width = acts.shape[2]
    wg = w_gate[0, 0]
    wu = w_up[0, 0]
    wd = w_down[0, 0]
    local_hidden = wg.shape[1]
    inv_ff = 1.0 / math.sqrt(FF)
    ticks = MB + sections - 1
    inputs = acts[0].reshape(MB, TOK, local_width)
    cots = cotangent[0].reshape(MB, TOK, local_width)
    saved = jnp.zeros((MB, TOK, D), jnp.bfloat16)
    gate_saved = jnp.zeros((MB, TOK, local_hidden), jnp.float32)
    upper_saved = jnp.zeros((MB, TOK, local_hidden), jnp.float32)
    out_buf = jnp.zeros((MB, TOK, local_width), jnp.bfloat16)
    incoming = jnp.zeros((TOK, local_width), jnp.bfloat16)
    for tick in range(ticks):
        micro = tick - section
        valid = (micro >= 0) & (micro < MB)
        place = jnp.clip(micro, 0, MB - 1)
        first = lax.dynamic_index_in_dim(inputs, place, 0, keepdims=False)
        x_local = jnp.where(section == 0, first, incoming)
        x_full = widen(x_local)
        xf, rms, normed, normed_b, gate, upper = forward_parts(x_full, wg, wu)
        hidden = (jax.nn.silu(gate) * upper).astype(jnp.bfloat16)
        partial_out = jnp.dot(hidden, wd, preferred_element_type=jnp.float32) * inv_ff
        share = lax.psum_scatter(
            partial_out.astype(jnp.bfloat16), "tp", scatter_dimension=1, tiled=True
        ).astype(jnp.float32)
        y_local = (x_local.astype(jnp.float32) + share).astype(jnp.bfloat16)
        if tick < ticks - 1:
            incoming = passed_along(y_local, "section", 1)
        saved = jnp.where(valid, lax.dynamic_update_index_in_dim(saved, x_full, place, 0), saved)
        gate_saved = jnp.where(
            valid, lax.dynamic_update_index_in_dim(gate_saved, gate, place, 0), gate_saved
        )
        upper_saved = jnp.where(
            valid, lax.dynamic_update_index_in_dim(upper_saved, upper, place, 0), upper_saved
        )
        out_buf = jnp.where(
            valid, lax.dynamic_update_index_in_dim(out_buf, y_local, place, 0), out_buf
        )
    acc_gate = jnp.zeros(wg.shape, jnp.float32)
    acc_up = jnp.zeros(wu.shape, jnp.float32)
    acc_down = jnp.zeros(wd.shape, jnp.float32)
    grad_buf = jnp.zeros((MB, TOK, local_width), jnp.bfloat16)
    incoming_back = jnp.zeros((TOK, local_width), jnp.bfloat16)
    for tick in range(ticks):
        micro = tick - (sections - 1 - section)
        valid = (micro >= 0) & (micro < MB)
        place = jnp.clip(micro, 0, MB - 1)
        last_cot = lax.dynamic_index_in_dim(cots, place, 0, keepdims=False)
        dy_local = jnp.where(section == sections - 1, last_cot, incoming_back)
        dy_full = widen(dy_local)
        x_full = lax.dynamic_index_in_dim(saved, place, 0, keepdims=False)
        xf, rms, normed, normed_b = norm_parts(x_full)
        gate = lax.dynamic_index_in_dim(gate_saved, place, 0, keepdims=False)
        upper = lax.dynamic_index_in_dim(upper_saved, place, 0, keepdims=False)
        sig = jax.nn.sigmoid(gate)
        active = gate * sig
        hidden = (active * upper).astype(jnp.bfloat16)
        dh = contract(dy_full, wd, 1, 1) * inv_ff
        dgate = (dh * upper * sig * (1.0 + gate * (1.0 - sig))).astype(jnp.bfloat16)
        dup = (dh * active).astype(jnp.bfloat16)
        acc_down = acc_down + jnp.where(valid, contract(hidden, dy_full, 0, 0) * inv_ff, 0.0)
        acc_gate = acc_gate + jnp.where(
            valid, contract(normed_b, dgate, 0, 0) * (1.0 / math.sqrt(D)), 0.0
        )
        acc_up = acc_up + jnp.where(
            valid, contract(normed_b, dup, 0, 0) * (1.0 / math.sqrt(D)), 0.0
        )
        partial_in = (contract(dgate, wg, 1, 1) + contract(dup, wu, 1, 1)) * (1.0 / math.sqrt(D))
        dnorm_local = lax.psum_scatter(
            partial_in.astype(jnp.bfloat16), "tp", scatter_dimension=1, tiled=True
        ).astype(jnp.float32)
        normed_local = lax.dynamic_slice_in_dim(normed, part * local_width, local_width, 1)
        stat = lax.psum(jnp.sum(dnorm_local * normed_local, axis=1), "tp") / D
        dx_local = (
            dy_local.astype(jnp.float32) + (dnorm_local - normed_local * stat[:, None]) / rms
        ).astype(jnp.bfloat16)
        grad_buf = jnp.where(
            valid, lax.dynamic_update_index_in_dim(grad_buf, dx_local, place, 0), grad_buf
        )
        if tick < ticks - 1:
            incoming_back = passed_along(dx_local, "section", -1)
    new_gate_local = adam_step(wg, m_gate[0, 0], v_gate[0, 0], acc_gate)
    new_up_local = adam_step(wu, m_up[0, 0], v_up[0, 0], acc_up)
    new_down_local = adam_step(wd, m_down[0, 0], v_down[0, 0], acc_down)
    flat_size = wg.shape[0] * wg.shape[1]
    stacked = jnp.stack(
        [
            new_gate_local.reshape(flat_size),
            new_up_local.reshape(flat_size),
            new_down_local.reshape(flat_size),
        ]
    )
    levels = lax.axis_size("rep").bit_length() - 1
    branches = [functools.partial(partner_mean, distance=2**level) for level in range(levels)]
    which = steps[0] % levels
    averaged = lax.switch(which, branches, stacked)
    new_gate = averaged[0].reshape(wg.shape)[None, None]
    new_up = averaged[1].reshape(wu.shape)[None, None]
    new_down = averaged[2].reshape(wd.shape)[None, None]
    section_out = out_buf.reshape(1, 1, MB * TOK, local_width)
    section_in_grad = grad_buf.reshape(1, 1, MB * TOK, local_width)
    return (section_out, section_in_grad, new_gate, new_up, new_down)


def solution(mesh):
    return jax.shard_map(
        on_device,
        mesh=mesh,
        in_specs=(
            P("rep", None, "tp"),
            P("rep", None, "tp"),
            P("section", "rep", None, "tp"),
            P("section", "rep", None, "tp"),
            P("section", "rep", "tp", None),
            P("section", "rep", None, "tp"),
            P("section", "rep", None, "tp"),
            P("section", "rep", "tp", None),
            P("section", "rep", None, "tp"),
            P("section", "rep", None, "tp"),
            P("section", "rep", "tp", None),
            P("section"),
        ),
        out_specs=(
            P("section", "rep", None, "tp"),
            P("section", "rep", None, "tp"),
            P("section", "rep", None, "tp"),
            P("section", "rep", None, "tp"),
            P("section", "rep", "tp", None),
        ),
        check_vma=False,
    )
```

profile of v0, /device:TPU:32, one launch (start us, length us, event | category | flops | bytes accessed | tf_op | source)
XLA Modules:
  0.0 1533.5 jit_solution(6093599195167706535)
XLA Ops:
  9.0 45.2 %all-gather = bf16[1,128,896]{1,2,0:T(8,128)(2,1)S(1)} all-gather(bf16[1,128,112]{1,2,0:T(8,128)(2,1)S(1)} %copy_select_fusion.1), channel_id=2, replica_groups=mesh['section'=4,'rep'=8,'tp'=8] {'tp'}, dimensions={2}, use_global_device_ids=true | all-gather | bytes 258048 | tf_op jit(solution)/shard_map/all_gather | solution.py:38
  60.3 77.0 %reduce-scatter.11.cloned.1.call-done = bf16[128,112]{0,1:T(8,128)(2,1)} async-done(((bf16[128,896]{0,1:T(8,128)(2,1)}), bf16[128,112]{0,1:T(8,128)(2,1)}) %reduce-scatter.11.cloned.1.call-update) | async-done | bytes 28688 | tf_op jit(solution)/shard_map/reduce_scatter | solution.py:109
  140.6 3.2 collective-permute-done.3
  143.8 44.1 %all_gather.31 = bf16[128,896]{0,1:T(8,128)(2,1)S(1)} all-gather(bf16[128,112]{0,1:T(8,128)(2,1)S(1)} %bitcast_select_fusion.19), channel_id=1, replica_groups=mesh['section'=4,'rep'=8,'tp'=8] {'tp'}, dimensions={1}, use_global_device_ids=true | all-gather | bytes 258048 | tf_op jit(solution)/shard_map/all_gather | solution.py:38
  192.2 72.5 %reduce-scatter.13.cloned.1.call-done = bf16[128,112]{0,1:T(8,128)(2,1)} async-done(((bf16[128,896]{0,1:T(8,128)(2,1)}), bf16[128,112]{0,1:T(8,128)(2,1)}) %reduce-scatter.13.cloned.1.call-update) | async-done | bytes 28688 | tf_op jit(solution)/shard_map/reduce_scatter | solution.py:109
  271.3 44.1 %all_gather.32 = bf16[128,896]{0,1:T(8,128)(2,1)S(1)} all-gather(bf16[128,112]{0,1:T(8,128)(2,1)S(1)} %bitcast_select_fusion.18), channel_id=1, replica_groups=mesh['section'=4,'rep'=8,'tp'=8] {'tp'}, dimensions={1}, use_global_device_ids=true | all-gather | bytes 258048 | tf_op jit(solution)/shard_map/all_gather | solution.py:38
  320.4 71.8 %reduce-scatter.15.cloned.1.call-done = bf16[128,112]{0,1:T(8,128)(2,1)} async-done(((bf16[128,896]{0,1:T(8,128)(2,1)}), bf16[128,112]{0,1:T(8,128)(2,1)}) %reduce-scatter.15.cloned.1.call-update) | async-done | bytes 28688 | tf_op jit(solution)/shard_map/reduce_scatter | solution.py:109
  395.6 46.2 %all-gather.1 = bf16[1,128,896]{1,2,0:T(8,128)(2,1)} all-gather(bf16[1,128,112]{1,2,0:T(8,128)(2,1)} %copy_select_fusion), channel_id=3, replica_groups=mesh['section'=4,'rep'=8,'tp'=8] {'tp'}, dimensions={2}, use_global_device_ids=true | all-gather | bytes 258048 | tf_op jit(solution)/shard_map/all_gather | solution.py:38
  443.4 44.0 %all_gather.33 = bf16[128,896]{0,1:T(8,128)(2,1)S(1)} all-gather(bf16[128,112]{0,1:T(8,128)(2,1)S(1)} %bitcast_select_fusion.17), channel_id=1, replica_groups=mesh['section'=4,'rep'=8,'tp'=8] {'tp'}, dimensions={1}, use_global_device_ids=true | all-gather | bytes 258048 | tf_op jit(solution)/shard_map/all_gather | solution.py:38
  492.7 72.0 %reduce-scatter.17.cloned.1.call-done = bf16[128,112]{0,1:T(8,128)(2,1)} async-done(((bf16[128,896]{0,1:T(8,128)(2,1)}), bf16[128,112]{0,1:T(8,128)(2,1)}) %reduce-scatter.17.cloned.1.call-update) | async-done | bytes 28688 | tf_op jit(solution)/shard_map/reduce_scatter | solution.py:109
  572.2 44.5 %all_gather.34 = bf16[128,896]{0,1:T(8,128)(2,1)S(1)} all-gather(bf16[128,112]{0,1:T(8,128)(2,1)S(1)} %bitcast_select_fusion.16), channel_id=1, replica_groups=mesh['section'=4,'rep'=8,'tp'=8] {'tp'}, dimensions={1}, use_global_device_ids=true | all-gather | bytes 258048 | tf_op jit(solution)/shard_map/all_gather | solution.py:38
  631.1 2.8 fusion.139
  635.5 65.6 %reduce-scatter.21.cloned.1.call-done = bf16[128,112]{0,1:T(8,128)(2,1)} async-done(((bf16[128,896]{0,1:T(8,128)(2,1)}), bf16[128,112]{0,1:T(8,128)(2,1)}) %reduce-scatter.21.cloned.1.call-update) | async-done | bytes 28688 | tf_op jit(solution)/shard_map/reduce_scatter | solution.py:155
  702.0 26.7 %psum.35 = f32[128]{0:T(128)S(1)} all-reduce(f32[128]{0:T(128)S(1)} %fusion.173), channel_id=1, replica_groups=mesh['section'=4,'rep'=8,'tp'=8] {'tp'}, use_global_device_ids=true, to_apply=%region_13.14 | all-reduce | flops 128 | bytes 1024 | tf_op jit(solution)/shard_map/psum | solution.py:159
  729.6 3.0 collective-permute-start.7
  732.6 45.2 %reduce-scatter.19.cloned.1.call-done = bf16[128,112]{0,1:T(8,128)(2,1)} async-done(((bf16[128,896]{0,1:T(8,128)(2,1)}), bf16[128,112]{0,1:T(8,128)(2,1)}) %reduce-scatter.19.cloned.1.call-update) | async-done | bytes 28688 | tf_op jit(solution)/shard_map/reduce_scatter | solution.py:109
  780.7 44.0 %all_gather.36 = bf16[128,896]{0,1:T(8,128)(2,1)S(1)} all-gather(bf16[128,112]{0,1:T(8,128)(2,1)S(1)} %bitcast_select_fusion.15), channel_id=1, replica_groups=mesh['section'=4,'rep'=8,'tp'=8] {'tp'}, dimensions={1}, use_global_device_ids=true | all-gather | bytes 258048 | tf_op jit(solution)/shard_map/all_gather | solution.py:38
  829.0 2.8 fusion.165
  831.8 2.9 fusion.143
  834.7 67.0 %reduce-scatter.23.cloned.1.call-done = bf16[128,112]{0,1:T(8,128)(2,1)} async-done(((bf16[128,896]{0,1:T(8,128)(2,1)}), bf16[128,112]{0,1:T(8,128)(2,1)}) %reduce-scatter.23.cloned.1.call-update) | async-done | bytes 28688 | tf_op jit(solution)/shard_map/reduce_scatter | solution.py:155
  902.6 26.7 %psum.36 = f32[128]{0:T(128)S(1)} all-reduce(f32[128]{0:T(128)S(1)} %fusion.177), channel_id=1, replica_groups=mesh['section'=4,'rep'=8,'tp'=8] {'tp'}, use_global_device_ids=true, to_apply=%region_17.18 | all-reduce | flops 128 | bytes 1024 | tf_op jit(solution)/shard_map/psum | solution.py:159
  930.2 3.0 collective-permute-start.8
  933.2 2.8 fusion.167
  936.6 44.2 %all_gather.37 = bf16[128,896]{0,1:T(8,128)(2,1)S(1)} all-gather(bf16[128,112]{0,1:T(8,128)(2,1)S(1)} %bitcast_select_fusion.14), channel_id=1, replica_groups=mesh['section'=4,'rep'=8,'tp'=8] {'tp'}, dimensions={1}, use_global_device_ids=true | all-gather | bytes 258048 | tf_op jit(solution)/shard_map/all_gather | solution.py:38
  987.6 2.8 fusion.145
  990.4 69.3 %reduce-scatter.25.cloned.1.call-done = bf16[128,112]{0,1:T(8,128)(2,1)} async-done(((bf16[128,896]{0,1:T(8,128)(2,1)}), bf16[128,112]{0,1:T(8,128)(2,1)}) %reduce-scatter.25.cloned.1.call-update) | async-done | bytes 28688 | tf_op jit(solution)/shard_map/reduce_scatter | solution.py:155
  1060.6 26.7 %psum.37 = f32[128]{0:T(128)S(1)} all-reduce(f32[128]{0:T(128)S(1)} %fusion.181), channel_id=1, replica_groups=mesh['section'=4,'rep'=8,'tp'=8] {'tp'}, use_global_device_ids=true, to_apply=%region_21.22 | all-reduce | flops 128 | bytes 1024 | tf_op jit(solution)/shard_map/psum | solution.py:159
  1088.2 3.0 collective-permute-start.9
  1094.6 44.4 %all_gather.38 = bf16[128,896]{0,1:T(8,128)(2,1)S(1)} all-gather(bf16[128,112]{0,1:T(8,128)(2,1)S(1)} %bitcast_select_fusion.13), channel_id=1, replica_groups=mesh['section'=4,'rep'=8,'tp'=8] {'tp'}, dimensions={1}, use_global_device_ids=true | all-gather | bytes 258048 | tf_op jit(solution)/shard_map/all_gather | solution.py:38
  1145.8 2.9 fusion.147
  1148.6 69.2 %reduce-scatter.27.cloned.1.call-done = bf16[128,112]{0,1:T(8,128)(2,1)} async-done(((bf16[128,896]{0,1:T(8,128)(2,1)}), bf16[128,112]{0,1:T(8,128)(2,1)}) %reduce-scatter.27.cloned.1.call-update) | async-done | bytes 28688 | tf_op jit(solution)/shard_map/reduce_scatter | solution.py:155
  1218.7 26.7 %psum.38 = f32[128]{0:T(128)S(1)} all-reduce(f32[128]{0:T(128)S(1)} %fusion.185), channel_id=1, replica_groups=mesh['section'=4,'rep'=8,'tp'=8] {'tp'}, use_global_device_ids=true, to_apply=%region_25.26 | all-reduce | flops 128 | bytes 1024 | tf_op jit(solution)/shard_map/psum | solution.py:159
  1246.3 3.0 collective-permute-start.10
  1252.1 44.2 %all_gather.39 = bf16[128,896]{0,1:T(8,128)(2,1)S(1)} all-gather(bf16[128,112]{0,1:T(8,128)(2,1)S(1)} %bitcast_select_fusion.12), channel_id=1, replica_groups=mesh['section'=4,'rep'=8,'tp'=8] {'tp'}, dimensions={1}, use_global_device_ids=true | all-gather | bytes 258048 | tf_op jit(solution)/shard_map/all_gather | solution.py:38
  1299.9 7.5 fusion.21
  1307.5 3.1 copy.51
  1310.6 3.9 fusion.19
  1319.3 12.1 stack_reshape.10
  1331.4 5.0 fusion.20
  1337.8 4.0 reshape.169
  1341.8 11.3 stack_reshape.9
  1353.2 7.8 pad_maximum_fusion
  1361.0 138.3 %conditional.2 = (bf16[3,544768]{1,0:T(4,128)(2,1)}, bf16[1,544768]{1,0:T(2,128)(2,1)}, bf16[1,544768]{1,0:T(2,128)(2,1)}, bf16[1,544768]{1,0:T(2,128)(2,1)}, bf...) conditional(s32[]{:T(128)} %clamp.3, ...), branch_computations={%region_30.31_spmd, %region_31.32_spmd, %region_32.33_spmd} | conditional | flops 8171520 | bytes 56655996
  1362.1 10.6 collective-permute-start.2
  1372.7 81.9 %collective-permute-done.2 = bf16[3,544768]{1,0:T(4,128)(2,1)S(1)} collective-permute-done((bf16[3,544768]{1,0:T(4,128)(2,1)S(1)}, bf16[3,544768]{1,0:T(4,128)(2,1)S(1)}, u32[]{:S(2)}, u32[]{:S(2)}) %collective-permute-start.2) | collective-permute-done | bytes 3268640 | tf_op jit(solution)/shard_map/cond/branch_2_fun/ppermute | solution.py:28
  1454.7 2.9 add_multiply_fusion.2
  1457.6 32.6 %fusion.237 = (bf16[544768]{0:T(1024)(128)(2,1)S(1)}, bf16[1,544768]{1,0:T(2,128)(2,1)}, bf16[544768]{0:T(1024)(128)(2,1)}, bf16[1,544768]{1,0:T(2,128)(2,1)}, b...) fusion(bf16[3,544768]{1,0:T(4,128)(2,1)S(1)} %add_multiply_fusion.2), kind=kLoop, calls=%fused_computation.386 | loop fusion | bytes 9805824 | tf_op jit(solution)/shard_map/slice | solution.py:185
  1500.4 24.5 %psum.39 = f32[128]{0:T(128)S(1)} all-reduce(f32[128]{0:T(128)S(1)} %fusion.189), channel_id=1, replica_groups=mesh['section'=4,'rep'=8,'tp'=8] {'tp'}, use_global_device_ids=true, to_apply=%region_29.30 | all-reduce | flops 128 | bytes 1024 | tf_op jit(solution)/shard_map/psum | solution.py:159
  (257 shorter events, 115.6 us)
Async XLA Ops:
  7.2 130.1 %reduce-scatter.11.cloned.1.call-start = ((), (), s32[]{:S(2)}) async-start(), calls=%async_computation.10 | async-start | bytes 258048 | tf_op jit(solution)/shard_map/reduce_scatter | solution.py:109
  60.2 128.3 %copy-start.3 = (bf16[1,1,896,608]{2,3,1,0:T(8,128)(2,1)S(1)}, bf16[1,1,896,608]{2,3,1,0:T(8,128)(2,1)}, u32[]{:S(2)}) copy-start(bf16[1,1,896,608]{2,3,1,0:T(8,128)(2,1)} %param.18) | copy-start | bytes 3268612
  60.3 204.5 %reduce-scatter.13.cloned.1.call-start = ((), (), s32[]{:S(2)}) async-start(), calls=%async_computation.11 | async-start | bytes 258048 | tf_op jit(solution)/shard_map/reduce_scatter | solution.py:109
  138.1 5.8 collective-permute-start.3
  192.1 200.1 %reduce-scatter.15.cloned.1.call-start = ((), (), s32[]{:S(2)}) async-start(), calls=%async_computation.12 | async-start | bytes 258048 | tf_op jit(solution)/shard_map/reduce_scatter | solution.py:109
  265.5 5.8 collective-permute-start.4
  269.1 50.5 %copy-start.26 = (bf16[1,128,112]{1,0,2:T(2,128)(2,1)}, bf16[1,128,112]{1,0,2:T(2,128)(2,1)S(1)}, u32[]{:S(2)}) copy-start(bf16[1,128,112]{1,0,2:T(2,128)(2,1)S(1)} %get-tuple-element.116) | copy-start | bytes 86020
  271.3 47.0 %copy-start.34 = (bf16[128,112]{0,1:T(8,128)(2,1)}, bf16[128,112]{0,1:T(8,128)(2,1)S(1)}, u32[]{:S(2)}) copy-start(bf16[128,112]{0,1:T(8,128)(2,1)S(1)} %bitcast_select_fusion.18) | copy-start | bytes 86020
  319.6 245.2 %reduce-scatter.17.cloned.1.call-start = ((), (), s32[]{:S(2)}) async-start(), calls=%async_computation.13 | async-start | bytes 258048 | tf_op jit(solution)/shard_map/reduce_scatter | solution.py:109
  393.0 49.5 %collective-permute-start.5 = (bf16[128,112]{0,1:T(8,128)(2,1)S(1)}, bf16[128,112]{0,1:T(8,128)(2,1)S(1)}, u32[]{:S(2)}, u32[]{:S(2)}) collective-permute-start(bf16[128,112]{0,1:T(8,128)(2,1)S(1)} %get-tuple-element.80), channel_id=1, source_target_pairs={{0,64},{64,128},{128,192},{1,65},{65,129},{129,193},{2,66},{66,130... | collective-permute-start | bytes 86024 | tf_op jit(solution)/shard_map/ppermute | solution.py:34
  443.3 44.2 %copy-start.33 = (bf16[128,112]{0,1:T(8,128)(2,1)}, bf16[128,112]{0,1:T(8,128)(2,1)S(1)}, u32[]{:S(2)}) copy-start(bf16[128,112]{0,1:T(8,128)(2,1)S(1)} %bitcast_select_fusion.17) | copy-start | bytes 86020
  491.6 209.5 %reduce-scatter.21.cloned.1.call-start = ((), (), s32[]{:S(2)}) async-start(), calls=%async_computation.15 | async-start | bytes 258048 | tf_op jit(solution)/shard_map/reduce_scatter | solution.py:155
  565.6 53.4 %copy-start.18 = (bf16[2,128,112]{1,2,0:T(8,128)(2,1)}, bf16[2,128,112]{1,2,0:T(8,128)(2,1)S(1)}, u32[]{:S(2)}) copy-start(bf16[2,128,112]{1,2,0:T(8,128)(2,1)S(1)} %get-tuple-element.77) | copy-start | bytes 172036
  565.6 5.8 collective-permute-start.6
  572.2 44.6 %copy-start.28 = (bf16[128,112]{0,1:T(8,128)(2,1)}, bf16[128,112]{0,1:T(8,128)(2,1)S(1)}, u32[]{:S(2)}) copy-start(bf16[128,112]{0,1:T(8,128)(2,1)S(1)} %bitcast_select_fusion.16) | copy-start | bytes 86020
  623.4 10.7 copy-start.43
  623.4 10.7 copy-start.44
  628.3 149.5 %reduce-scatter.19.cloned.1.call-start = ((), (), s32[]{:S(2)}) async-start(), calls=%async_computation.14 | async-start | bytes 258048 | tf_op jit(solution)/shard_map/reduce_scatter | solution.py:109
  634.0 94.7 %copy-start.27 = (bf16[1,128,112]{1,0,2:T(2,128)(2,1)S(1)}, bf16[1,128,112]{1,0,2:T(2,128)(2,1)}, u32[]{:S(2)}) copy-start(bf16[1,128,112]{1,0,2:T(2,128)(2,1)} %copy-done.26) | copy-start | bytes 86020
  634.0 143.8 %copy-start.19 = (bf16[2,128,112]{1,2,0:T(8,128)(2,1)S(1)}, bf16[2,128,112]{1,2,0:T(8,128)(2,1)}, u32[]{:S(2)}) copy-start(bf16[2,128,112]{1,2,0:T(8,128)(2,1)} %copy-done.18) | copy-start | bytes 172036
  634.0 143.8 %copy-start.29 = (bf16[128,112]{0,1:T(8,128)(2,1)S(1)}, bf16[128,112]{0,1:T(8,128)(2,1)}, u32[]{:S(2)}) copy-start(bf16[128,112]{0,1:T(8,128)(2,1)} %copy-done.28) | copy-start | bytes 86020
  634.0 145.3 %copy-start.39 = (bf16[1,128,112]{1,0,2:T(2,128)(2,1)S(1)}, bf16[1,128,112]{1,0,2:T(2,128)(2,1)}, u32[]{:S(2)}) copy-start(bf16[1,128,112]{1,0,2:T(2,128)(2,1)} %get-tuple-element.115) | copy-start | bytes 86020
  634.0 267.7 %reduce-scatter.23.cloned.1.call-start = ((), (), s32[]{:S(2)}) async-start(), calls=%async_computation.16 | async-start | bytes 258048 | tf_op jit(solution)/shard_map/reduce_scatter | solution.py:155
  729.6 49.7 %collective-permute-start.7 = (bf16[128,112]{0,1:T(8,128)(2,1)S(1)}, bf16[128,112]{0,1:T(8,128)(2,1)}, u32[]{:S(2)}, u32[]{:S(2)}) collective-permute-start(bf16[128,112]{0,1:T(8,128)(2,1)S(1)} %get-tuple-element.76), channel_id=1, source_target_pairs={{64,0},{128,64},{192,128},{65,1},{129,65},{193,129},{66,2},{130,66... | collective-permute-start | bytes 86024 | tf_op jit(solution)/shard_map/ppermute | solution.py:34
  829.0 230.7 %reduce-scatter.25.cloned.1.call-start = ((), (), s32[]{:S(2)}) async-start(), calls=%async_computation.17 | async-start | bytes 258048 | tf_op jit(solution)/shard_map/reduce_scatter | solution.py:155
  834.7 101.3 %copy-start.38 = (bf16[1,128,112]{1,0,2:T(2,128)(2,1)S(1)}, bf16[1,128,112]{1,0,2:T(2,128)(2,1)}, u32[]{:S(2)}) copy-start(bf16[1,128,112]{1,0,2:T(2,128)(2,1)} %get-tuple-element.114) | copy-start | bytes 86020
  929.3 51.6 %copy-start.55 = (bf16[1,1,608,896]{3,2,1,0:T(8,128)(2,1)S(1)}, bf16[1,1,608,896]{3,2,1,0:T(8,128)(2,1)}, u32[]{:S(2)}) copy-start(bf16[1,1,608,896]{3,2,1,0:T(8,128)(2,1)} %param.19) | copy-start | bytes 3268612
  930.2 5.8 collective-permute-start.8
  984.9 232.9 %reduce-scatter.27.cloned.1.call-start = ((), (), s32[]{:S(2)}) async-start(), calls=%async_computation.18 | async-start | bytes 258048 | tf_op jit(solution)/shard_map/reduce_scatter | solution.py:155
  990.4 103.5 %copy-start.37 = (bf16[1,128,112]{1,0,2:T(2,128)(2,1)S(1)}, bf16[1,128,112]{1,0,2:T(2,128)(2,1)}, u32[]{:S(2)}) copy-start(bf16[1,128,112]{1,0,2:T(2,128)(2,1)} %get-tuple-element.113) | copy-start | bytes 86020
  1087.2 51.7 %copy-start.56 = (bf16[1,1,608,896]{3,2,1,0:T(8,128)(2,1)S(1)}, bf16[1,1,608,896]{3,2,1,0:T(8,128)(2,1)}, u32[]{:S(2)}) copy-start(bf16[1,1,608,896]{3,2,1,0:T(8,128)(2,1)} %param.19) | copy-start | bytes 3268612
  1088.2 5.8 collective-permute-start.9
  1143.0 356.4 %reduce-scatter.29.cloned.1.call-start = ((), (), s32[]{:S(2)}) async-start(), calls=%async_computation.19 | async-start | bytes 258048 | tf_op jit(solution)/shard_map/reduce_scatter | solution.py:155
  1148.6 103.5 %copy-start.36 = (bf16[1,128,112]{1,0,2:T(2,128)(2,1)S(1)}, bf16[1,128,112]{1,0,2:T(2,128)(2,1)}, u32[]{:S(2)}) copy-start(bf16[1,128,112]{1,0,2:T(2,128)(2,1)} %get-tuple-element.112) | copy-start | bytes 86020
  1245.4 51.0 %copy-start.57 = (bf16[1,1,608,896]{3,2,1,0:T(8,128)(2,1)S(1)}, bf16[1,1,608,896]{3,2,1,0:T(8,128)(2,1)}, u32[]{:S(2)}) copy-start(bf16[1,1,608,896]{3,2,1,0:T(8,128)(2,1)} %param.19) | copy-start | bytes 3268612
  1246.3 5.8 collective-permute-start.10
  1299.9 10.7 copy-start.9
  1299.9 10.7 copy-start.10
  1299.9 10.7 copy-start.11
  1299.9 10.7 copy-start.58
  1299.9 10.7 copy-start.59
  1319.3 12.1 copy-start.7
  1319.3 12.1 copy-start.60
  1337.8 15.3 copy-start.6
  1341.8 11.4 copy-start.5
  1362.1 92.6 %collective-permute-start.2 = (bf16[3,544768]{1,0:T(4,128)(2,1)S(1)}, bf16[3,544768]{1,0:T(4,128)(2,1)S(1)}, u32[]{:S(2)}, u32[]{:S(2)}) collective-permute-start(bf16[3,544768]{1,0:T(4,128)(2,1)S(1)} %param.2), channel_id=1, source_target_pairs={{0,32},{8,40},{16,48},{24,56},{32,0},{40,8},{48,16},{56,24},{1,33}... | collective-permute-start | bytes 9805832 | tf_op jit(solution)/shard_map/cond/branch_2_fun/ppermute | solution.py:28
  1457.6 32.6 %copy-start.2 = (bf16[3,544768]{1,0:T(4,128)(2,1)}, bf16[3,544768]{1,0:T(4,128)(2,1)S(1)}, u32[]{:S(2)}) copy-start(bf16[3,544768]{1,0:T(4,128)(2,1)S(1)} %add_multiply_fusion.2) | copy-start | bytes 9805828 | tf_op jit(solution)/shard_map/conditional
  1499.4 27.1 %copy-start.16 = (bf16[1,1,896,608]{2,3,1,0:T(8,128)(2,1)}, bf16[1,1,896,608]{2,3,1,0:T(8,128)(2,1)S(1)}, u32[]{:S(2)}) copy-start(bf16[1,1,896,608]{2,3,1,0:T(8,128)(2,1)S(1)} %get-tuple-element.44) | copy-start | bytes 3268612
  (30 other events, 61.5 us)
Sparse Core Ops, SparseCore 0:
  60.4 76.8 reduce-scatter.10
  192.2 72.4 reduce-scatter.12
  319.7 72.4 reduce-scatter.14
  491.7 73.0 reduce-scatter.16
  628.4 72.6 reduce-scatter.20
  704.6 73.1 reduce-scatter.18
  829.1 72.5 reduce-scatter.22
  985.0 74.6 reduce-scatter.24
  1143.1 74.6 reduce-scatter.26
  1300.0 74.5 reduce-scatter.28
where the time goes:
time: 1540 us; the launch traced here: 1530 us
  waiting for transfers between devices  699 us (45%)
  blocking collectives  576 us (37%)
  local copies, waits for them, and re-layouts  88.1 us (6%)
  matrix products  87.2 us (6%)
  starting transfers between devices  33.3 us (2%)
  other arithmetic  32.1 us (2%)
  between operations  16 us (1%)
    all_gather x10, blocking collectives, widen(): return lax.all_gather(value, 'tp', axis=1, tiled=True)  445 us
    reduce_scatter x5, waiting for transfers between devices, on_device(): lax.psum_scatter(partial_out.astype(jnp.bfloat16), 'tp', scatter_dimensio...  339 us
    reduce_scatter x5, waiting for transfers between devices, on_device(): lax.psum_scatter(partial_in.astype(jnp.bfloat16), 'tp', scatter_dimension...  271 us
    psum x5, blocking collectives, on_device(): stat = lax.psum(jnp.sum(dnorm_local * normed_local, axis=1), 'tp') / D  131 us
    ppermute x1, waiting for transfers between devices, from_behind(): lax.ppermute(array, axis, [(i, (i + by) % peers) for i in range(peers)])  81.9 us
    dot_general x30, matrix products, contract(): lax.dot_general(left, right, (((left_dim,), (right_dim,)), ((), ())), pre...  64.8 us
    slice x1, local copies, waits for them, and re-layouts, on_device(): new_down = averaged[2].reshape(wd.shape)[None, None]  32.6 us
  transfers between devices with their start and end apart: 19, of which 13 were waited for; matrix products, arithmetic and copies ran while one was open for 9% of the time, Pallas kernels for 0%

commit v1 on v0

v1 whole, which is shorter than its diff:
```python
import functools
import math

import jax
import jax.numpy as jnp
from jax import lax
from jax.experimental import pallas as pl
from jax.experimental.pallas import tpu as pltpu
from jax.sharding import PartitionSpec as P

D = 896
FF = 4864
ROWS = 256
SECTIONS = 4
TP = 8
NX = 4
BLOCK = D // TP
MB = 2
R = ROWS // MB
C = R // NX

NORM_EPS = 1e-06
ADAM_EPS = 1e-08
LEARN = 0.3
BETA_ONE = 0.9
BETA_TWO = 0.95
INV_D = 1.0 / math.sqrt(D)
INV_FF = 1.0 / math.sqrt(FF)
MESH = pl.DeviceIdType.MESH
BF16 = jnp.bfloat16
F32 = jnp.float32

CODES = {"I": 0, "H": 1, "M": 2, "T": 3, "h": 4, "m": 5, "t": 6, "O": 7, "o": 8, "E": 9}


def plan(text):
    return [(CODES[name], int(mb)) for name, mb in zip(text[::2], text[1::2])]


EARLY = plan("I0H0M0H1T0M1T1O0O1h0m0h1t0m1t1o0o1E0")
LAST = plan("I0H0M0m0H1M1t0m1t1T0T1O0O1o0o1E0E1E1")


def rms_parts(rows):
    xf = rows.astype(F32)
    rms = jnp.sqrt(jnp.mean(xf * xf, axis=1, keepdims=True) + NORM_EPS)
    return xf, rms


def dot_nn(left, right):
    return lax.dot_general(left, right, (((1,), (0,)), ((), ())), preferred_element_type=F32)


def dot_nt(left, right):
    return lax.dot_general(left, right, (((1,), (1,)), ((), ())), preferred_element_type=F32)


def chain_kernel(
    acts,
    cot,
    wg,
    wu,
    wd,
    out_y,
    out_dx,
    out_nb,
    out_hidden,
    out_dgate,
    out_dup,
    out_dy,
    xin,
    full,
    act_s,
    slope_s,
    spread,
    nb,
    dyb,
    xrow,
    dyrow,
    part_f,
    part_b,
    rs_f,
    rs_b,
    zsend_f,
    zsend_b,
    zrecv_f,
    zrecv_b,
    zown_f,
    zown_b,
    ost_f,
    ost_b,
    orecv_f,
    orecv_b,
    in_send,
    in_recv,
    ag_send,
    ag_recv,
    rs_send,
    rs_recv,
    z_send,
    z_recv,
    o_send,
    o_recv,
):
    s = lax.axis_index("section")
    t = lax.axis_index("tp")
    h = t // NX
    x = t % NX
    own = pl.ds(pl.multiple_of(x * C, C), C)

    def at_tp(where):
        return {"tp": where}

    def peer_x(k):
        return (x + k) % NX

    barrier = pltpu.get_barrier_semaphore()
    for k in range(1, TP):
        pl.semaphore_signal(barrier, inc=1, device_id={"tp": (t + k) % TP}, device_id_type=MESH)
    for step in (1, SECTIONS - 1):
        for hh in range(2):
            pl.semaphore_signal(
                barrier,
                inc=1,
                device_id={"section": (s + step) % SECTIONS, "tp": hh * NX + x},
                device_id_type=MESH,
            )
    pl.semaphore_wait(barrier, TP - 1 + 4)

    def in_copy(src, k):
        return pltpu.make_async_remote_copy(
            src_ref=src,
            dst_ref=xin.at[t],
            send_sem=in_send.at[k],
            recv_sem=in_recv.at[t],
            device_id={"tp": (t + k) % TP},
            device_id_type=MESH,
        )

    def in_wait(k):
        who = (t + k) % TP
        pltpu.make_async_remote_copy(
            src_ref=xin.at[who],
            dst_ref=xin.at[who],
            send_sem=in_send.at[0],
            recv_sem=in_recv.at[who],
            device_id={"tp": who},
            device_id_type=MESH,
        ).wait_recv()

    order = (4, 5, 3, 6, 2, 7, 1)

    @pl.when(s == 0)
    def _():
        for k in order:
            in_copy(acts, k).start()

    @pl.when(s == SECTIONS - 1)
    def _():
        for k in order:
            in_copy(cot, k).start()

    def gather_blocks():
        for k in range(1, TP):
            in_wait(k)
        full[...] = jnp.concatenate([xin[k] for k in range(TP)], axis=1)

    def ag_copy(buf, kind, mb, k):
        return pltpu.make_async_remote_copy(
            src_ref=buf.at[mb, own],
            dst_ref=buf.at[mb, own],
            send_sem=ag_send.at[kind, mb, k],
            recv_sem=ag_recv.at[kind, mb, NX - k],
            device_id={"tp": h * NX + peer_x(k)},
            device_id_type=MESH,
        )

    def ag_wait(buf, kind, mb, k):
        rows = pl.ds(pl.multiple_of(peer_x(k) * C, C), C)
        pltpu.make_async_remote_copy(
            src_ref=buf.at[mb, rows],
            dst_ref=buf.at[mb, rows],
            send_sem=ag_send.at[kind, mb, k],
            recv_sem=ag_recv.at[kind, mb, k],
            device_id={"tp": h * NX + peer_x(k)},
            device_id_type=MESH,
        ).wait_recv()

    def rs_copy(part, buf, kind, mb, k):
        rows = pl.ds(pl.multiple_of(peer_x(k) * C, C), C)
        return pltpu.make_async_remote_copy(
            src_ref=part.at[mb, rows],
            dst_ref=buf.at[mb, NX - k],
            send_sem=rs_send.at[kind, mb, k],
            recv_sem=rs_recv.at[kind, mb, NX - k],
            device_id={"tp": h * NX + peer_x(k)},
            device_id_type=MESH,
        )

    def rs_wait(part, buf, kind, mb, k):
        rows = pl.ds(pl.multiple_of(peer_x(k) * C, C), C)
        pltpu.make_async_remote_copy(
            src_ref=part.at[mb, rows],
            dst_ref=buf.at[mb, k],
            send_sem=rs_send.at[kind, mb, k],
            recv_sem=rs_recv.at[kind, mb, k],
            device_id={"tp": h * NX + peer_x(k)},
            device_id_type=MESH,
        ).wait_recv()

    def z_copy(src, buf, kind, mb, hh):
        to = s + 1 if kind == 0 else s - 1
        return pltpu.make_async_remote_copy(
            src_ref=src.at[mb],
            dst_ref=buf.at[mb, h],
            send_sem=z_send.at[kind, mb, hh],
            recv_sem=z_recv.at[kind, mb, h],
            device_id={"section": to % SECTIONS, "tp": hh * NX + x},
            device_id_type=MESH,
        )

    def z_wait(src, buf, kind, mb, hh):
        pltpu.make_async_remote_copy(
            src_ref=src.at[mb],
            dst_ref=buf.at[mb, hh],
            send_sem=z_send.at[kind, mb, hh],
            recv_sem=z_recv.at[kind, mb, hh],
            device_id={"tp": (1 - h) * NX + x},
            device_id_type=MESH,
        ).wait_recv()

    def zown_copy(src, buf, kind, mb):
        return pltpu.make_async_remote_copy(
            src_ref=src.at[mb],
            dst_ref=buf.at[mb],
            send_sem=z_send.at[kind, mb, 2],
            recv_sem=z_recv.at[kind, mb, 2],
            device_id={"tp": (1 - h) * NX + x},
            device_id_type=MESH,
        )

    def o_copy(ost, orecv, kind, mb, k):
        return pltpu.make_async_remote_copy(
            src_ref=ost.at[mb, peer_x(k)],
            dst_ref=orecv.at[mb, x],
            send_sem=o_send.at[kind, mb, k],
            recv_sem=o_recv.at[kind, mb, NX - k],
            device_id={"tp": h * NX + peer_x(k)},
            device_id_type=MESH,
        )

    def o_wait(ost, orecv, kind, mb, k):
        pltpu.make_async_remote_copy(
            src_ref=ost.at[mb, peer_x(k)],
            dst_ref=orecv.at[mb, peer_x(k)],
            send_sem=o_send.at[kind, mb, k],
            recv_sem=o_recv.at[kind, mb, k],
            device_id={"tp": h * NX + peer_x(k)},
            device_id_type=MESH,
        ).wait_recv()

    far_first = (2, 1, 3)

    def step_first(mb):
        @pl.when(s == 0)
        def _():
            xin[t] = acts[...]
            gather_blocks()
            for b in range(MB):
                xf, rms = rms_parts(full[b * R : (b + 1) * R])
                nb[b] = (xf / rms).astype(BF16)
                xrow[b] = full[pl.ds(pl.multiple_of(b * R + x * C, C), C), :]

        @pl.when(s == SECTIONS - 1)
        def _():
            xin[t] = cot[...]
            gather_blocks()
            for b in range(MB):
                dyb[b] = full[b * R : (b + 1) * R]
                dyrow[b] = full[pl.ds(pl.multiple_of(b * R + x * C, C), C), :]

    def head_fwd(mb):
        @pl.when(s > 0)
        def _():
            z_wait(zsend_f, zrecv_f, 0, mb, 0)
            z_wait(zsend_f, zrecv_f, 0, mb, 1)
            rows = (zrecv_f[mb, 0].astype(F32) + zrecv_f[mb, 1].astype(F32)).astype(BF16)
            xrow[mb] = rows
            xf, rms = rms_parts(rows)
            nb[mb, own] = (xf / rms).astype(BF16)
            for k in far_first:
                ag_copy(nb, 0, mb, k).start()

    def main_fwd(mb):
        @pl.when(s > 0)
        def _():
            for k in (1, 3, 2):
                ag_wait(nb, 0, mb, k)

        normed = nb[mb]
        gate = dot_nn(normed, wg[...]) * INV_D
        upper = dot_nn(normed, wu[...]) * INV_D
        sig = jax.nn.sigmoid(gate)
        active = gate * sig
        hidden = (active * upper).astype(BF16)
        part_f[mb] = (dot_nn(hidden, wd[...]) * INV_FF).astype(BF16)
        for k in far_first:
            rs_copy(part_f, rs_f, 0, mb, k).start()
        rows = pl.ds(pl.multiple_of(mb * R, R), R)
        out_hidden[rows, :] = hidden
        act_s[mb] = active
        slope_s[mb] = upper * sig * (1.0 + gate * (1.0 - sig))

    def half_sum(part, buf, kind, mb):
        for k in (1, 3, 2):
            rs_wait(part, buf, kind, mb, k)
        total = part[mb, own].astype(F32)
        for k in range(1, NX):
            total = total + buf[mb, k].astype(F32)
        return total

    def tail_fwd(mb):
        half = half_sum(part_f, rs_f, 0, mb)
        zsend_f[mb] = (half + 0.5 * xrow[mb].astype(F32)).astype(BF16)

        @pl.when(s < SECTIONS - 1)
        def _():
            z_copy(zsend_f, zrecv_f, 0, mb, 0).start()
            z_copy(zsend_f, zrecv_f, 0, mb, 1).start()

        zown_copy(zsend_f, zown_f, 0, mb).start()

    def head_bwd(mb):
        @pl.when(s < SECTIONS - 1)
        def _():
            z_wait(zsend_b, zrecv_b, 1, mb, 0)
            z_wait(zsend_b, zrecv_b, 1, mb, 1)
            rows = (zrecv_b[mb, 0].astype(F32) + zrecv_b[mb, 1].astype(F32)).astype(BF16)
            dyrow[mb] = rows
            dyb[mb, own] = rows
            for k in far_first:
                ag_copy(dyb, 1, mb, k).start()

    def main_bwd(mb):
        @pl.when(s < SECTIONS - 1)
        def _():
            for k in (1, 3, 2):
                ag_wait(dyb, 1, mb, k)

        dh = dot_nt(dyb[mb], wd[...]) * INV_FF
        dgate = (dh * slope_s[mb]).astype(BF16)
        dup = (dh * act_s[mb]).astype(BF16)
        part_b[mb] = ((dot_nt(dgate, wg[...]) + dot_nt(dup, wu[...])) * INV_D).astype(BF16)
        for k in far_first:
            rs_copy(part_b, rs_b, 1, mb, k).start()
        rows = pl.ds(pl.multiple_of(mb * R, R), R)
        out_dgate[rows, :] = dgate
        out_dup[rows, :] = dup

    def tail_bwd(mb):
        xf, rms = rms_parts(xrow[mb])
        normed = xf / rms
        half = half_sum(part_b, rs_b, 1, mb)
        stat = jnp.sum(half * normed, axis=1, keepdims=True) / D
        grad = 0.5 * dyrow[mb].astype(F32) + (half - normed * stat) / rms
        zsend_b[mb] = grad.astype(BF16)

        @pl.when(s > 0)
        def _():
            z_copy(zsend_b, zrecv_b, 1, mb, 0).start()
            z_copy(zsend_b, zrecv_b, 1, mb, 1).start()

        zown_copy(zsend_b, zown_b, 1, mb).start()

    def spread_columns(zsend, zown, ost, orecv, kind, mb):
        zown_copy(zsend, zown, kind, mb).wait_recv()
        rows = (zsend[mb].astype(F32) + zown[mb].astype(F32)).astype(BF16)
        wide = dot_nn(rows, spread[...]).astype(BF16)
        for q in range(NX):
            ost[mb, q] = wide[:, q * 128 : (q + 1) * 128]
        orecv[mb, x] = ost[mb, x]
        for k in far_first:
            o_copy(ost, orecv, kind, mb, k).start()

    def out_fwd(mb):
        @pl.when(mb == 0)
        def _():
            feature = lax.broadcasted_iota(jnp.int32, (D, NX * 128), 0) - h * (NX * BLOCK)
            place = lax.broadcasted_iota(jnp.int32, (D, NX * 128), 1)
            lane = place % 128
            hit = (feature == (place // 128) * BLOCK + lane) & (lane < BLOCK)
            spread[...] = jnp.where(hit, 1.0, 0.0).astype(BF16)

        spread_columns(zsend_f, zown_f, ost_f, orecv_f, 0, mb)

    def out_bwd(mb):
        spread_columns(zsend_b, zown_b, ost_b, orecv_b, 1, mb)

    def finish(mb):
        @pl.when(mb == 0)
        def _():
            for b in range(MB):
                out_nb[b * R : (b + 1) * R, :] = nb[b]
                out_dy[b * R : (b + 1) * R, :] = dyb[b]
                for kind, ost, orecv, out in ((0, ost_f, orecv_f, out_y), (1, ost_b, orecv_b, out_dx)):
                    for k in (1, 3, 2):
                        o_wait(ost, orecv, kind, b, k)
                    for j in range(NX):
                        rows = slice(b * R + j * C, b * R + (j + 1) * C)
                        out[rows, :] = orecv[b, j][:, :BLOCK]

    steps = {
        0: step_first,
        1: head_fwd,
        2: main_fwd,
        3: tail_fwd,
        4: head_bwd,
        5: main_bwd,
        6: tail_bwd,
        7: out_fwd,
        8: out_bwd,
        9: finish,
    }

    def run(index, carry):
        last = s == SECTIONS - 1
        code = jnp.int32(0)
        mb = jnp.int32(0)
        for place in range(len(EARLY)):
            here = index == place
            code = jnp.where(here, jnp.where(last, LAST[place][0], EARLY[place][0]), code)
            mb = jnp.where(here, jnp.where(last, LAST[place][1], EARLY[place][1]), mb)
        for number, step in steps.items():

            @pl.when(code == number)
            def _(step=step):
                step(mb)

        return carry

    lax.fori_loop(0, len(EARLY), run, 0)

    @pl.when(s == 0)
    def _():
        for k in order:
            in_copy(acts, k).wait_send()

    @pl.when(s == SECTIONS - 1)
    def _():
        for k in order:
            in_copy(cot, k).wait_send()

    def drain(mb, carry):
        for k in far_first:
            rs_copy(part_f, rs_f, 0, mb, k).wait_send()
            rs_copy(part_b, rs_b, 1, mb, k).wait_send()
            o_copy(ost_f, orecv_f, 0, mb, k).wait_send()
            o_copy(ost_b, orecv_b, 1, mb, k).wait_send()
        zown_copy(zsend_f, zown_f, 0, mb).wait_send()
        zown_copy(zsend_b, zown_b, 1, mb).wait_send()

        @pl.when(s > 0)
        def _():
            for k in far_first:
                ag_copy(nb, 0, mb, k).wait_send()
            for hh in range(2):
                z_copy(zsend_b, zrecv_b, 1, mb, hh).wait_send()

        @pl.when(s < SECTIONS - 1)
        def _():
            for k in far_first:
                ag_copy(dyb, 1, mb, k).wait_send()
            for hh in range(2):
                z_copy(zsend_f, zrecv_f, 0, mb, hh).wait_send()

        return carry

    lax.fori_loop(0, MB, drain, 0)


def chain(acts, cot, wg, wu, wd):
    hid = wg.shape[1]
    vm = pl.BlockSpec(memory_space=pltpu.VMEM)
    shape = jax.ShapeDtypeStruct
    dma = pltpu.SemaphoreType.DMA
    return pl.pallas_call(
        chain_kernel,
        out_shape=(
            shape((ROWS, BLOCK), BF16),
            shape((ROWS, BLOCK), BF16),
            shape((ROWS, D), BF16),
            shape((ROWS, hid), BF16),
            shape((ROWS, hid), BF16),
            shape((ROWS, hid), BF16),
            shape((ROWS, D), BF16),
        ),
        in_specs=[vm] * 5,
        out_specs=[vm] * 7,
        scratch_shapes=[
            pltpu.VMEM((TP, ROWS, BLOCK), BF16),
            pltpu.VMEM((ROWS, D), BF16),
            pltpu.VMEM((MB, R, hid), F32),
            pltpu.VMEM((MB, R, hid), F32),
            pltpu.VMEM((D, NX * 128), BF16),
            pltpu.VMEM((MB, R, D), BF16),
            pltpu.VMEM((MB, R, D), BF16),
            pltpu.VMEM((MB, C, D), BF16),
            pltpu.VMEM((MB, C, D), BF16),
            pltpu.VMEM((MB, R, D), BF16),
            pltpu.VMEM((MB, R, D), BF16),
            pltpu.VMEM((MB, NX, C, D), BF16),
            pltpu.VMEM((MB, NX, C, D), BF16),
            pltpu.VMEM((MB, C, D), BF16),
            pltpu.VMEM((MB, C, D), BF16),
            pltpu.VMEM((MB, 2, C, D), BF16),
            pltpu.VMEM((MB, 2, C, D), BF16),
            pltpu.VMEM((MB, C, D), BF16),
            pltpu.VMEM((MB, C, D), BF16),
            pltpu.VMEM((MB, NX, C, 128), BF16),
            pltpu.VMEM((MB, NX, C, 128), BF16),
            pltpu.VMEM((MB, NX, C, 128), BF16),
            pltpu.VMEM((MB, NX, C, 128), BF16),
            dma((TP,)),
            dma((TP,)),
            dma((2, MB, NX)),
            dma((2, MB, NX)),
            dma((2, MB, NX)),
            dma((2, MB, NX)),
            dma((2, MB, 3)),
            dma((2, MB, 3)),
            dma((2, MB, NX)),
            dma((2, MB, NX)),
        ],
        compiler_params=pltpu.CompilerParams(
            collective_id=0, has_side_effects=True, vmem_limit_bytes=48 * 1024 * 1024
        ),
        name="chain",
    )(acts, cot, wg, wu, wd)


def contract_rows(left, right):
    return lax.dot_general(left, right, (((0,), (0,)), ((), ())), preferred_element_type=F32)


def adam_step(weight, first, second, grad):
    m_new = BETA_ONE * first.astype(F32) + (1.0 - BETA_ONE) * grad
    v_new = BETA_TWO * second.astype(F32) + (1.0 - BETA_TWO) * grad * grad
    return (weight.astype(F32) - LEARN * m_new / (jnp.sqrt(v_new) + ADAM_EPS)).astype(BF16)


def gossip(*updated, distance):
    peers = lax.axis_size("rep")
    pairs = [(i, (i + distance) % peers) for i in range(peers)]
    return tuple(
        ((own.astype(F32) + lax.ppermute(own, "rep", pairs).astype(F32)) * 0.5).astype(BF16)
        for own in updated
    )


def on_device(
    acts, cotangent, w_gate, w_up, w_down, m_gate, m_up, m_down, v_gate, v_up, v_down, steps
):
    wg, wu, wd = w_gate[0, 0], w_up[0, 0], w_down[0, 0]
    y, dx, nb, hidden, dgate, dup, dy = chain(acts[0], cotangent[0], wg, wu, wd)
    new_down = adam_step(wd, m_down[0, 0], v_down[0, 0], contract_rows(hidden, dy) * INV_FF)
    new_gate = adam_step(wg, m_gate[0, 0], v_gate[0, 0], contract_rows(nb, dgate) * INV_D)
    new_up = adam_step(wu, m_up[0, 0], v_up[0, 0], contract_rows(nb, dup) * INV_D)
    levels = lax.axis_size("rep").bit_length() - 1
    branches = [functools.partial(gossip, distance=2**level) for level in range(levels)]
    new_down, new_gate, new_up = lax.switch(
        steps[0] % levels, branches, new_down, new_gate, new_up
    )
    return (
        y[None, None],
        dx[None, None],
        new_gate[None, None],
        new_up[None, None],
        new_down[None, None],
    )


def solution(mesh):
    return jax.shard_map(
        on_device,
        mesh=mesh,
        in_specs=(
            P("rep", None, "tp"),
            P("rep", None, "tp"),
            P("section", "rep", None, "tp"),
            P("section", "rep", None, "tp"),
            P("section", "rep", "tp", None),
            P("section", "rep", None, "tp"),
            P("section", "rep", None, "tp"),
            P("section", "rep", "tp", None),
            P("section", "rep", None, "tp"),
            P("section", "rep", None, "tp"),
            P("section", "rep", "tp", None),
            P("section"),
        ),
        out_specs=(
            P("section", "rep", None, "tp"),
            P("section", "rep", None, "tp"),
            P("section", "rep", None, "tp"),
            P("section", "rep", None, "tp"),
            P("section", "rep", "tp", None),
        ),
        check_vma=False,
    )
```

time: 1540 us -> 209 us (0.14)
  the two profiles are of different devices: /device:TPU:32 before, /device:TPU:2 now
where the time goes in v1:
time: 209 us; the launch traced here: 208 us
  Pallas kernels  137 us (66%)
  waiting for transfers between devices  34.4 us (16%)
  local copies, waits for them, and re-layouts  20.5 us (10%)
  matrix products  10.5 us (5%)
  other arithmetic  2.58 us (1%)
    pallas_call x1, Pallas kernels, chain(): pl.pallas_call(chain_kernel, out_shape=(shape((ROWS, BLOCK), BF16), shape...  137 us
    ppermute x3, waiting for transfers between devices, gossip(): lax.ppermute(own, 'rep', pairs).astype(F32)  34.4 us
    unnamed x48, local copies, waits for them, and re-layouts  17.1 us
    dot_general x3, matrix products, contract_rows(): lax.dot_general(left, right, (((0,), (0,)), ((), ())), preferred_element_...  10.5 us
  transfers between devices with their start and end apart: 3, of which 3 were waited for; matrix products, arithmetic and copies ran while one was open for 2% of the time, Pallas kernels for 0%

profile of v1, /device:TPU:2, one launch (start us, length us, event | category | flops | bytes accessed | tf_op | source)
XLA Modules:
  0.0 208.2 jit_solution(860760263737600856)
XLA Ops:
  1.3 0.9 copy.35
  2.2 0.9 copy.36
  3.2 0.0 copy-start.20
  3.2 2.1 %copy.37 = bf16[1,1,896,608]{3,2,1,0:T(8,128)(2,1)S(1)} copy(bf16[1,1,896,608]{2,3,1,0:T(8,128)(2,1)} %param.17) | data formatting | bytes 2179072 | tf_op args[2]
  5.3 0.0 copy-done.20
  5.3 1.1 copy.38
  6.5 0.0 copy-start.21
  6.5 2.5 %copy.39 = bf16[1,1,896,608]{3,2,1,0:T(8,128)(2,1)} copy(bf16[1,1,896,608]{2,3,1,0:T(8,128)(2,1)} %param.20) | data formatting | bytes 2179072 | tf_op args[5]
  9.0 0.0 copy-done.21
  9.0 1.4 copy.44
  10.4 2.4 %copy.41 = bf16[1,1,896,608]{3,2,1,0:T(8,128)(2,1)} copy(bf16[1,1,896,608]{2,3,1,0:T(8,128)(2,1)} %param.23) | data formatting | bytes 2179072 | tf_op args[8]
  12.7 2.5 %copy.46 = bf16[1,1,896,608]{3,2,1,0:T(8,128)(2,1)} copy(bf16[1,1,896,608]{2,3,1,0:T(8,128)(2,1)} %param.24) | data formatting | bytes 2179072 | tf_op args[9]
  15.2 0.0 copy-done
  15.2 137.0 %chain.1 = (bf16[256,112]{1,0:T(8,128)(2,1)S(1)}, bf16[256,112]{1,0:T(8,128)(2,1)S(1)}, bf16[256,896]{1,0:T(8,128)(2,1)S(1)}, bf16[256,608]{1,0:T(8,128)(2,1)S(1...) custom-call(bf16[256,112]{1,0:T(8,128)(2,1)S(1)} %bitcast.98, ...), custom_call_target="tpu_custom_call" | custom-call | tf_op jit(solution)/shard_map/chain/pallas_call | solution.py:486
  152.3 0.0 copy-start.1
  152.3 0.0 copy-start.3
  152.3 0.0 copy-start.5
  152.3 0.0 copy-start.7
  152.4 3.0 %fusion.20 = bf16[896,608]{1,0:T(8,128)(2,1)} fusion(bf16[1,1,896,608]{3,2,1,0:T(8,128)(2,1)S(1)} %copy-done.16, bf16[1,1,896,608]{3,2,1,0:T(8,128)(2,1)S(1)} %copy-done.15, bf16[256,896]{1,0:T(8,128)(2,1)S(1)} %get-tuple-element.49, bf16[256,608]{1,0:T(8,128)(2,1)S(1)} %get-tuple-element.51, bf16[1,1,896,608]{3,2,1,0:T(8,128)(2,1)S(1)} %copy.38), kind=kOutput, calls=%fused_computation.33 | convolution fusion | flops 287637504 | bytes 5128192 | tf_op jit(solution)/shard_map/dot_general | solution.py:542
  155.3 0.0 copy-done.5
  155.3 0.0 copy-start.4
  155.4 0.0 copy-start.2
  155.4 0.0 copy-start.6
  155.4 0.0 copy-start.8
  155.4 3.0 %fusion.19 = bf16[896,608]{1,0:T(8,128)(2,1)} fusion(bf16[1,1,896,608]{3,2,1,0:T(8,128)(2,1)S(1)} %copy-done.14, bf16[1,1,896,608]{3,2,1,0:T(8,128)(2,1)S(1)} %copy-done.13, bf16[256,896]{1,0:T(8,128)(2,1)S(1)} %get-tuple-element.49, bf16[256,608]{1,0:T(8,128)(2,1)S(1)} %get-tuple-element.50, bf16[1,1,896,608]{3,2,1,0:T(8,128)(2,1)S(1)} %copy.37), kind=kOutput, calls=%fused_computation.32 | convolution fusion | flops 287637504 | bytes 5128192 | tf_op jit(solution)/shard_map/dot_general | solution.py:542
  158.4 0.7 copy.55
  159.1 0.0 copy-done.2
  159.1 0.7 copy.56
  159.8 0.0 copy-done.8
  159.8 4.5 %fusion.26 = bf16[608,896]{1,0:T(8,128)(2,1)} fusion(bf16[1,1,608,896]{3,2,1,0:T(8,128)(2,1)} %param.25, bf16[1,1,608,896]{3,2,1,0:T(8,128)(2,1)} %param.22, bf16[256,608]{1,0:T(8,128)(2,1)S(1)} %copy-done.8, bf16[256,896]{1,0:T(8,128)(2,1)S(1)} %copy-done.6, bf16[1,1,608,896]{3,2,1,0:T(8,128)(2,1)S(1)} %copy-done), kind=kOutput, calls=%fused_computation.41 | convolution fusion | flops 287637504 | bytes 5128192 | tf_op jit(solution)/shard_map/dot_general | solution.py:542
  164.4 42.1 %conditional.1 = (bf16[1,1,608,896]{3,2,1,0:T(8,128)(2,1)S(1)}, bf16[1,1,896,608]{2,3,1,0:T(8,128)(2,1)S(1)}, bf16[1,1,896,608]{2,3,1,0:T(8,128)(2,1)S(1)}) conditional(s32[]{:T(128)} %clamp.3, (bf16[608,896]{1,0:T(8,128)(2,1)}, bf16[896,608]{1,0:T(8,128)(2,1)}, bf16[896,608]{1,0:T(8,128)(2,1)S(1)}) %tuple.39, ...), branch_computations={%region_0.1_spmd, %region_1.2_spmd, %region_2.3_spmd} | conditional | flops 8171520 | bytes 31596716 | solution.py:570
  164.4 2.3 %copy.49 = bf16[896,608]{0,1:T(8,128)(2,1)} copy(bf16[896,608]{1,0:T(8,128)(2,1)} %get-tuple-element.61) | data formatting | bytes 2179072 | tf_op jit(solution)/shard_map
  166.7 0.0 collective-permute-start.1
  166.7 1.1 copy.50
  167.8 1.6 collective-permute-start.2
  169.4 0.0 collective-permute-start
  169.5 13.4 %collective-permute-done.1 = bf16[896,608]{0,1:T(8,128)(2,1)} collective-permute-done((bf16[896,608]{0,1:T(8,128)(2,1)}, bf16[896,608]{0,1:T(8,128)(2,1)}, u32[]{:S(2)}, u32[]{:S(2)}) %collective-permute-start.1) | collective-permute-done | bytes 1089568 | tf_op jit(solution)/shard_map/cond/branch_0_fun/ppermute | solution.py:555
  182.9 1.9 fusion.1
  184.8 9.7 %collective-permute-done.2 = bf16[896,608]{0,1:T(8,128)(2,1)S(1)} collective-permute-done((bf16[896,608]{0,1:T(8,128)(2,1)S(1)}, bf16[896,608]{0,1:T(8,128)(2,1)S(1)}, u32[]{:S(2)}, u32[]{:S(2)}) %collective-permute-start.2) | collective-permute-done | bytes 1089568 | tf_op jit(solution)/shard_map/cond/branch_0_fun/ppermute | solution.py:555
  194.5 0.3 fusion.2
  194.8 11.3 %collective-permute-done = bf16[608,896]{1,0:T(8,128)(2,1)S(1)} collective-permute-done((bf16[608,896]{1,0:T(8,128)(2,1)S(1)}, bf16[608,896]{1,0:T(8,128)(2,1)S(1)}, u32[]{:S(2)}, u32[]{:S(2)}) %collective-permute-start) | collective-permute-done | bytes 1089568 | tf_op jit(solution)/shard_map/cond/branch_0_fun/ppermute | solution.py:555
  206.2 0.3 fusion
  206.5 0.0 copy-start.17
  206.5 0.0 copy-start.18
  206.5 0.0 copy-start.19
  206.5 0.9 copy-done.17
  207.5 0.4 copy-done.18
  207.8 0.4 copy-done.19
  (18 shorter events, 0.0 us)
Async XLA Ops:
  3.2 2.2 %copy-start.20 = (bf16[1,1,896,608]{2,3,1,0:T(8,128)(2,1)S(1)}, bf16[1,1,896,608]{2,3,1,0:T(8,128)(2,1)}, u32[]{:S(2)}) copy-start(bf16[1,1,896,608]{2,3,1,0:T(8,128)(2,1)} %param.18) | copy-start | bytes 3268612
  6.5 2.5 %copy-start.21 = (bf16[1,1,896,608]{2,3,1,0:T(8,128)(2,1)S(1)}, bf16[1,1,896,608]{2,3,1,0:T(8,128)(2,1)}, u32[]{:S(2)}) copy-start(bf16[1,1,896,608]{2,3,1,0:T(8,128)(2,1)} %param.21) | copy-start | bytes 3268612
  12.7 2.5 %copy-start = (bf16[1,1,608,896]{3,2,1,0:T(8,128)(2,1)S(1)}, bf16[1,1,608,896]{3,2,1,0:T(8,128)(2,1)}, u32[]{:S(2)}) copy-start(bf16[1,1,608,896]{3,2,1,0:T(8,128)(2,1)} %param.19) | copy-start | bytes 3268612
  15.2 137.1 %copy-start.15 = (bf16[1,1,896,608]{3,2,1,0:T(8,128)(2,1)S(1)}, bf16[1,1,896,608]{3,2,1,0:T(8,128)(2,1)}, u32[]{:S(2)}) copy-start(bf16[1,1,896,608]{3,2,1,0:T(8,128)(2,1)} %copy.44) | copy-start | bytes 3268612
  15.2 137.1 %copy-start.16 = (bf16[1,1,896,608]{3,2,1,0:T(8,128)(2,1)S(1)}, bf16[1,1,896,608]{3,2,1,0:T(8,128)(2,1)}, u32[]{:S(2)}) copy-start(bf16[1,1,896,608]{3,2,1,0:T(8,128)(2,1)} %copy.46) | copy-start | bytes 3268612
  152.3 3.0 %copy-start.1 = (bf16[256,112]{1,0:T(8,128)(2,1)}, bf16[256,112]{1,0:T(8,128)(2,1)S(1)}, u32[]{:S(2)}) copy-start(bf16[256,112]{1,0:T(8,128)(2,1)S(1)} %get-tuple-element.46) | copy-start | bytes 172036
  152.3 3.0 %copy-start.3 = (bf16[256,112]{1,0:T(8,128)(2,1)}, bf16[256,112]{1,0:T(8,128)(2,1)S(1)}, u32[]{:S(2)}) copy-start(bf16[256,112]{1,0:T(8,128)(2,1)S(1)} %get-tuple-element.45) | copy-start | bytes 172036
  152.3 3.0 %copy-start.5 = (bf16[256,896]{1,0:T(8,128)(2,1)}, bf16[256,896]{1,0:T(8,128)(2,1)S(1)}, u32[]{:S(2)}) copy-start(bf16[256,896]{1,0:T(8,128)(2,1)S(1)} %get-tuple-element.48) | copy-start | bytes 1376260
  152.3 3.0 %copy-start.7 = (bf16[256,608]{1,0:T(8,128)(2,1)}, bf16[256,608]{1,0:T(8,128)(2,1)S(1)}, u32[]{:S(2)}) copy-start(bf16[256,608]{1,0:T(8,128)(2,1)S(1)} %get-tuple-element.47) | copy-start | bytes 933892
  152.3 3.0 %copy-start.13 = (bf16[1,1,896,608]{3,2,1,0:T(8,128)(2,1)S(1)}, bf16[1,1,896,608]{3,2,1,0:T(8,128)(2,1)}, u32[]{:S(2)}) copy-start(bf16[1,1,896,608]{3,2,1,0:T(8,128)(2,1)} %copy.39) | copy-start | bytes 3268612
  152.3 3.0 %copy-start.14 = (bf16[1,1,896,608]{3,2,1,0:T(8,128)(2,1)S(1)}, bf16[1,1,896,608]{3,2,1,0:T(8,128)(2,1)}, u32[]{:S(2)}) copy-start(bf16[1,1,896,608]{3,2,1,0:T(8,128)(2,1)} %copy.41) | copy-start | bytes 3268612
  155.3 3.0 %copy-start.4 = (bf16[256,112]{1,0:T(8,128)(2,1)S(1)}, bf16[256,112]{1,0:T(8,128)(2,1)}, u32[]{:S(2)}) copy-start(bf16[256,112]{1,0:T(8,128)(2,1)} %copy-done.3) | copy-start | bytes 172036
  155.4 3.7 %copy-start.2 = (bf16[256,112]{1,0:T(8,128)(2,1)S(1)}, bf16[256,112]{1,0:T(8,128)(2,1)}, u32[]{:S(2)}) copy-start(bf16[256,112]{1,0:T(8,128)(2,1)} %copy-done.1) | copy-start | bytes 172036
  155.4 4.5 %copy-start.6 = (bf16[256,896]{1,0:T(8,128)(2,1)S(1)}, bf16[256,896]{1,0:T(8,128)(2,1)}, u32[]{:S(2)}) copy-start(bf16[256,896]{1,0:T(8,128)(2,1)} %copy-done.5) | copy-start | bytes 1376260
  155.4 4.5 %copy-start.8 = (bf16[256,608]{1,0:T(8,128)(2,1)S(1)}, bf16[256,608]{1,0:T(8,128)(2,1)}, u32[]{:S(2)}) copy-start(bf16[256,608]{1,0:T(8,128)(2,1)} %copy-done.7) | copy-start | bytes 933892
  159.8 4.5 %copy-start.9 = (bf16[896,608]{1,0:T(8,128)(2,1)S(1)}, bf16[896,608]{1,0:T(8,128)(2,1)}, u32[]{:S(2)}) copy-start(bf16[896,608]{1,0:T(8,128)(2,1)} %fusion.20) | copy-start | bytes 3268612
  166.7 2.7 %copy-start.10 = (bf16[608,896]{1,0:T(8,128)(2,1)S(1)}, bf16[608,896]{1,0:T(8,128)(2,1)}, u32[]{:S(2)}) copy-start(bf16[608,896]{1,0:T(8,128)(2,1)} %get-tuple-element.21) | copy-start | bytes 3268612 | tf_op jit(solution)/shard_map/cond
  166.7 16.2 %collective-permute-start.1 = (bf16[896,608]{0,1:T(8,128)(2,1)}, bf16[896,608]{0,1:T(8,128)(2,1)}, u32[]{:S(2)}, u32[]{:S(2)}) collective-permute-start(bf16[896,608]{0,1:T(8,128)(2,1)} %copy.49), channel_id=1, source_target_pairs={{0,8},{8,16},{16,24},{24,32},{32,40},{40,48},{48,56},{56,0},{1,9},... | collective-permute-start | bytes 3268616 | tf_op jit(solution)/shard_map/cond/branch_0_fun/ppermute | solution.py:555
  167.8 26.6 %collective-permute-start.2 = (bf16[896,608]{0,1:T(8,128)(2,1)S(1)}, bf16[896,608]{0,1:T(8,128)(2,1)S(1)}, u32[]{:S(2)}, u32[]{:S(2)}) collective-permute-start(bf16[896,608]{0,1:T(8,128)(2,1)S(1)} %copy.50), channel_id=1, source_target_pairs={{0,8},{8,16},{16,24},{24,32},{32,40},{40,48},{48,56},{56,0},{1,9},... | collective-permute-start | bytes 3268616 | tf_op jit(solution)/shard_map/cond/branch_0_fun/ppermute | solution.py:555
  169.4 36.7 %collective-permute-start = (bf16[608,896]{1,0:T(8,128)(2,1)S(1)}, bf16[608,896]{1,0:T(8,128)(2,1)S(1)}, u32[]{:S(2)}, u32[]{:S(2)}) collective-permute-start(bf16[608,896]{1,0:T(8,128)(2,1)S(1)} %copy-done.10), channel_id=1, source_target_pairs={{0,8},{8,16},{16,24},{24,32},{32,40},{40,48},{48,56},{56,0},{1,9},... | collective-permute-start | bytes 3268616 | tf_op jit(solution)/shard_map/cond/branch_0_fun/ppermute | solution.py:555
  206.5 1.0 copy-start.17
  206.5 1.3 copy-start.18
  206.5 1.7 copy-start.19
